TPU v7x, 32 devices: a whole 2x2x4 slice. The times are simulated.
32 devices in a mesh: pipe: 8 (over z, core), expert: 4 (over y, x).
Axes of the slice: x: 2, y: 2, z: 4, core: 2. Of those that a mesh axis runs over, the one named last changes fastest.
Arguments:
- fwd_state: bfloat16 [8, 512, 3584], P('pipe', 'expert'), may hold values from -6 to 6
- bwd_cot: bfloat16 [8, 512, 3584], P('pipe', 'expert'), may hold values from -6 to 6
- saved_inputs: bfloat16 [2, 8, 512, 3584], P(None, 'pipe', 'expert'), may hold values from -6 to 6
- fwd_entry: bfloat16 [512, 3584], P('expert'), may hold values from -6 to 6
- bwd_entry: bfloat16 [512, 3584], P('expert'), may hold values from -6 to 6
- fwd_ids: int32 [2, 8, 512, 2], P(None, 'pipe', 'expert'), may hold values from 0 to 3, all different within a row; in each aligned block of 128 rows (0 to 127, 128 to 255, ..., all dimensions but the last counted through in order) at most 80 rows name the same one
- bwd_ids: int32 [2, 8, 512, 2], P(None, 'pipe', 'expert'), may hold values from 0 to 3, all different within a row; in each aligned block of 128 rows (0 to 127, 128 to 255, ..., all dimensions but the last counted through in order) at most 80 rows name the same one
- norm_gain: float32 [8, 3584], P('pipe'), may hold values from 0.1 to 1.9
- router: bfloat16 [8, 3584, 4], P('pipe'), may hold values from -0.09375 to 0.09375
- up_weight: bfloat16 [8, 4, 3584, 1024], P('pipe', 'expert'), may hold values from -0.09375 to 0.09375
- down_weight: bfloat16 [8, 4, 1024, 3584], P('pipe', 'expert'), may hold values from -0.1875 to 0.1875
Outputs:
- fwd_out: bfloat16 [2, 8, 512, 3584], P(None, 'pipe', 'expert')
- bwd_out: bfloat16 [2, 8, 512, 3584], P(None, 'pipe', 'expert')
Inputs may be any that keep to these rules, and one draw needn't show every extreme that they name: `fwd_ids`: the 2 ids of a token differ. Within the 128 tokens of one device (aligned blocks), no expert is named by more than 80 tokens, a bound that some block reaches. `bwd_ids`: as for fwd_ids.
All inputs are finite; a program needn't handle non-finite values.
Results may differ from a plain program's by a relative error of at most 0.0059.
Values may be sent and summed in bfloat16 or wider, within the bound.
A program may use at most 128 MiB of HBM per device.

v0:
```python
import jax
import jax.numpy as jnp
from jax import lax
from jax.sharding import PartitionSpec as P

EPSILON = 1e-06


def with_halo(cells, sides, width):
    for axis, dim in sides:
        count = lax.axis_size(axis)
        ends = count - 1
        head = lax.slice_in_dim(cells, 0, width, axis=dim)
        tail = lax.slice_in_dim(cells, cells.shape[dim] - width, cells.shape[dim], axis=dim)
        cells = jnp.concatenate(
            [
                lax.ppermute(tail, axis, [(i, (i + 1) % count) for i in range(ends)]),
                cells,
                lax.ppermute(head, axis, [((i + 1) % count, i) for i in range(ends)]),
            ],
            axis=dim,
        )
    return cells


def normalize(activation, gain_row):
    values = activation.astype(jnp.float32)
    inverse_rms = lax.rsqrt(jnp.mean(values * values, axis=-1, keepdims=True) + EPSILON)
    return ((values * inverse_rms * gain_row).astype(jnp.bfloat16), inverse_rms)


def gating(normed, routing, expert_ids):
    logits = jnp.dot(normed, routing, preferred_element_type=jnp.float32)
    probability = jax.nn.sigmoid(logits)
    picked = expert_ids[:, :, None] == jnp.arange(routing.shape[1], dtype=jnp.int32)[None, None, :]
    chosen = jnp.sum(jnp.where(picked, probability[:, None, :], 0.0), axis=-1)
    chosen_sum = jnp.sum(chosen, axis=-1, keepdims=True)
    return (chosen / chosen_sum, chosen, chosen_sum, picked)


def expert_forward(row_block, up_matrix, down_matrix):
    upward = jnp.dot(row_block, up_matrix, preferred_element_type=jnp.float32)
    hidden = (upward * jax.nn.sigmoid(upward)).astype(jnp.bfloat16)
    return jnp.dot(hidden, down_matrix, preferred_element_type=jnp.float32).astype(jnp.bfloat16)


def expert_backward(row_block, gradients, up_matrix, down_matrix):
    upward = jnp.dot(row_block, up_matrix, preferred_element_type=jnp.float32)
    sigmoid_up = jax.nn.sigmoid(upward)
    hidden = (upward * sigmoid_up).astype(jnp.bfloat16)
    outputs = jnp.dot(hidden, down_matrix, preferred_element_type=jnp.float32).astype(jnp.bfloat16)
    dhidden = lax.dot_general(
        gradients, down_matrix, (((1,), (1,)), ((), ())), preferred_element_type=jnp.float32
    )
    dupward = (dhidden * sigmoid_up * (1.0 + upward * (1.0 - sigmoid_up))).astype(jnp.bfloat16)
    dnormed = lax.dot_general(
        dupward, up_matrix, (((1,), (1,)), ((), ())), preferred_element_type=jnp.float32
    )
    return (outputs, dnormed.astype(jnp.bfloat16))


def slotting(expert_ids, experts, capacity):
    token_count, top_count = expert_ids.shape
    assignments = token_count * top_count
    flattened = expert_ids.reshape(assignments)
    onehot = (flattened[:, None] == jnp.arange(experts, dtype=jnp.int32)[None, :]).astype(jnp.int32)
    position = jnp.sum((jnp.cumsum(onehot, axis=0) - 1) * onehot, axis=1)
    destination = flattened * capacity + position
    matches = destination[None, :] == jnp.arange(experts * capacity, dtype=jnp.int32)[:, None]
    filled = jnp.any(matches, axis=1)
    source = jnp.sum(
        jnp.where(matches, jnp.arange(assignments, dtype=jnp.int32)[None, :], 0), axis=1
    )
    return (destination, source, filled)


def pack_rows(rows, source, filled, experts, capacity):
    taken = jnp.where(filled[:, None], rows[source], jnp.zeros((), rows.dtype))
    return taken.reshape(experts, capacity, rows.shape[-1])


def unpack_rows(returned, destination, token_count, top_count):
    model_width = returned.shape[-1]
    flattened = returned.reshape(-1, model_width)
    return flattened[destination].reshape(token_count, top_count, model_width)


def finish_from_gate(
    activation,
    cotangent,
    inverse_rms,
    gain_row,
    routing,
    gate_weight,
    chosen,
    chosen_sum,
    picked,
    gate_grad,
    expert_grad,
):
    cot_values = cotangent.astype(jnp.float32)
    chosen_grad = (
        gate_grad - jnp.sum(gate_grad * gate_weight, axis=-1, keepdims=True)
    ) / chosen_sum
    selected_grad = chosen_grad * chosen * (1.0 - chosen)
    logit_grad = jnp.sum(jnp.where(picked, selected_grad[:, :, None], 0.0), axis=1)
    router_part = jnp.dot(
        logit_grad, routing.astype(jnp.float32).T, precision=lax.Precision.HIGHEST
    )
    norm_grad = jnp.sum(expert_grad.astype(jnp.float32), axis=1) + router_part
    scaled_grad = norm_grad * gain_row
    values = activation.astype(jnp.float32)
    correction = jnp.mean(scaled_grad * values, axis=-1, keepdims=True)
    result = cot_values + inverse_rms * scaled_grad - values * inverse_rms**3 * correction
    return result.astype(jnp.bfloat16)


def per_device(
    fwd_state,
    bwd_cot,
    saved_inputs,
    fwd_entry,
    bwd_entry,
    fwd_ids,
    bwd_ids,
    norm_gain,
    router,
    up_weight,
    down_weight,
):
    section_index = lax.axis_index("pipe")
    section_count = lax.axis_size("pipe")
    gain_row = norm_gain[0]
    routing = router[0]
    up_matrix = up_weight[0, 0]
    down_matrix = down_weight[0, 0]
    experts = routing.shape[1]
    token_count = fwd_ids.shape[2]
    top_count = fwd_ids.shape[3]
    capacity = 5 * token_count * top_count // (4 * experts)
    forward_in = fwd_state[0]
    cotangent = bwd_cot[0]
    forward_list = []
    backward_list = []
    tick_total = saved_inputs.shape[0]
    for tick_number in range(tick_total):
        forward_route = fwd_ids[tick_number, 0]
        normed_f, inverse_f = normalize(forward_in, gain_row)
        gate_f, chosen_f, sum_f, picked_f = gating(normed_f, routing, forward_route)
        destination_f, source_f, filled_f = slotting(forward_route, experts, capacity)
        outgoing_f = pack_rows(normed_f, source_f // top_count, filled_f, experts, capacity)
        stored = saved_inputs[tick_number, 0]
        backward_route = bwd_ids[tick_number, 0]
        normed_b, inverse_b = normalize(stored, gain_row)
        gate_b, chosen_b, sum_b, picked_b = gating(normed_b, routing, backward_route)
        destination_b, source_b, filled_b = slotting(backward_route, experts, capacity)
        outgoing_b = pack_rows(normed_b, source_b // top_count, filled_b, experts, capacity)
        run_received = lax.all_to_all(outgoing_f, "expert", split_axis=0, concat_axis=0, tiled=True)
        run_sources, run_slot_count, run_model_width = run_received.shape
        run_outputs = expert_forward(
            run_received.reshape(run_sources * run_slot_count, run_model_width),
            up_matrix,
            down_matrix,
        )
        returned_f = lax.all_to_all(
            run_outputs.reshape(run_sources, run_slot_count, run_model_width),
            "expert",
            split_axis=0,
            concat_axis=0,
            tiled=True,
        )
        out_grad = (gate_b[:, :, None] * cotangent.astype(jnp.float32)[:, None, :]).astype(
            jnp.bfloat16
        )
        outgoing_g = pack_rows(
            out_grad.reshape(token_count * top_count, -1), source_b, filled_b, experts, capacity
        )
        row_block = lax.all_to_all(outgoing_b, "expert", split_axis=0, concat_axis=0, tiled=True)
        gradients = lax.all_to_all(outgoing_g, "expert", split_axis=0, concat_axis=0, tiled=True)
        sources, slot_count, model_width = row_block.shape
        outputs, dnormed = expert_backward(
            row_block.reshape(sources * slot_count, model_width),
            gradients.reshape(sources * slot_count, model_width),
            up_matrix,
            down_matrix,
        )
        returned_y = lax.all_to_all(
            outputs.reshape(sources, slot_count, model_width),
            "expert",
            split_axis=0,
            concat_axis=0,
            tiled=True,
        )
        returned_g = lax.all_to_all(
            dnormed.reshape(sources, slot_count, model_width),
            "expert",
            split_axis=0,
            concat_axis=0,
            tiled=True,
        )
        expert_out = unpack_rows(returned_y, destination_b, token_count, top_count)
        gate_grad = jnp.sum(
            cotangent.astype(jnp.float32)[:, None, :] * expert_out.astype(jnp.float32), axis=-1
        )
        expert_grad = unpack_rows(returned_g, destination_b, token_count, top_count)
        expert_f = unpack_rows(returned_f, destination_f, token_count, top_count)
        mixed = forward_in.astype(jnp.float32) + jnp.sum(
            gate_f[:, :, None] * expert_f.astype(jnp.float32), axis=1
        )
        forward_result = mixed.astype(jnp.bfloat16)
        backward_result = finish_from_gate(
            stored,
            cotangent,
            inverse_b,
            gain_row,
            routing,
            gate_b,
            chosen_b,
            sum_b,
            picked_b,
            gate_grad,
            expert_grad,
        )
        forward_list.append(forward_result)
        backward_list.append(backward_result)
        if tick_number + 1 < tick_total:
            boundary = jnp.stack([backward_result, forward_result])
            arrived = with_halo(boundary, (("pipe", 0),), 1)
            forward_in = jnp.where(section_index == 0, fwd_entry, arrived[0])
            cotangent = jnp.where(section_index == section_count - 1, bwd_entry, arrived[3])
    return (jnp.stack(forward_list)[:, None], jnp.stack(backward_list)[:, None])


def solution(mesh):
    placed = (
        P("pipe", "expert", None),
        P("pipe", "expert", None),
        P(None, "pipe", "expert", None),
        P("expert", None),
        P("expert", None),
        P(None, "pipe", "expert", None),
        P(None, "pipe", "expert", None),
        P("pipe", None),
        P("pipe", None, None),
        P("pipe", "expert", None, None),
        P("pipe", "expert", None, None),
    )
    return jax.shard_map(
        per_device,
        mesh=mesh,
        in_specs=placed,
        out_specs=(P(None, "pipe", "expert", None), P(None, "pipe", "expert", None)),
        check_vma=False,
    )
```

profile of v0, /device:TPU:0, one launch (start us, length us, event | category | flops | bytes accessed | tf_op | source)
XLA Modules:
  0.0 463.1 jit_solution(7880076902613271101)
XLA Ops:
  15.6 5.3 %all-to-all-start.5 = ((bf16[4,80,3584]{2,1,0:T(8,128)(2,1)}), bf16[4,80,3584]{2,1,0:T(8,128)(2,1)}, u32[]{:S(2)}, u32[]{:S(2)}) async-start(bf16[4,80,3584]{2,1,0:T(8,128)(2,1)} %broadcast_select_fusion.2), calls=%async_computation.5 | async-start | bytes 4587520 | tf_op jit(solution)/shard_map/all_to_all | solution.py:178
  32.1 16.7 %all-to-all-done.5 = bf16[4,80,3584]{2,1,0:T(8,128)(2,1)} async-done(((bf16[4,80,3584]{2,1,0:T(8,128)(2,1)}), bf16[4,80,3584]{2,1,0:T(8,128)(2,1)}, u32[]{:S(2)}, u32[]{:S(2)}) %all-to-all-start.5) | async-done | bytes 2293792 | tf_op jit(solution)/shard_map/all_to_all | solution.py:178
  48.8 4.7 %all-to-all-start = ((bf16[4,80,3584]{2,1,0:T(8,128)(2,1)}), bf16[4,80,3584]{2,1,0:T(8,128)(2,1)}, u32[]{:S(2)}, u32[]{:S(2)}) async-start(bf16[4,80,3584]{2,1,0:T(8,128)(2,1)} %broadcast_select_fusion.5), calls=%async_computation | async-start | bytes 4587520 | tf_op jit(solution)/shard_map/all_to_all | solution.py:158
  57.2 5.6 %mul.420 = f32[256,3584]{1,0:T(8,128)} reshape(f32[128,2,3584]{2,1,0:T(2,128)} %mul.419) | data formatting | bytes 7340032 | tf_op jit(solution)/shard_map/mul | solution.py:172
  62.8 6.3 %fusion.18 = f32[320,1024]{1,0:T(8,128)S(1)} fusion(bf16[320,3584]{1,0:T(8,128)(2,1)} %bitcast.38, bf16[1,1,3584,1024]{3,2,1,0:T(8,128)(2,1)} %param.20), kind=kOutput, calls=%fused_computation.30 | convolution fusion | flops 2348810240 | bytes 10944512 | tf_op jit(solution)/shard_map/dot_general | solution.py:48
  70.2 7.1 %fusion.36 = bf16[320,3584]{1,0:T(8,128)(2,1)} fusion(bf16[1,1,1024,3584]{3,2,1,0:T(8,128)(2,1)} %param.21, f32[320,1024]{1,0:T(8,128)S(1)} %fusion.18), kind=kOutput, calls=%fused_computation.40 | convolution fusion | flops 2351595520 | bytes 10944512 | tf_op jit(solution)/shard_map/dot_general | solution.py:51
  85.6 12.2 %fusion.30 = bf16[320,3584]{1,0:T(8,128)(2,1)} fusion(bf16[1,1,1024,3584]{3,2,1,0:T(8,128)(2,1)} %param.21, bf16[320,3584]{1,0:T(8,128)(2,1)} %bitcast.7, bf16[1,1,3584,1024]{3,2,1,0:T(8,128)(2,1)} %param.20), kind=kOutput, calls=%fused_computation.38 | convolution fusion | flops 4700405760 | bytes 19267584 | tf_op jit(solution)/shard_map/dot_general | solution.py:44
  97.8 12.6 %all-to-all-done.7 = bf16[4,80,3584]{2,1,0:T(8,128)(2,1)S(1)} async-done(((bf16[4,80,3584]{2,1,0:T(8,128)(2,1)}), bf16[4,80,3584]{2,1,0:T(8,128)(2,1)S(1)}, u32[]{:S(2)}, u32[]{:S(2)}) %all-to-all-start.7) | async-done | bytes 2293792 | tf_op jit(solution)/shard_map/all_to_all | solution.py:187
  110.4 4.9 %all-to-all-start.1 = ((bf16[4,80,3584]{2,1,0:T(8,128)(2,1)}), bf16[4,80,3584]{2,1,0:T(8,128)(2,1)}, u32[]{:S(2)}, u32[]{:S(2)}) async-start(bf16[4,80,3584]{2,1,0:T(8,128)(2,1)} %bitcast.324), calls=%async_computation.1 | async-start | bytes 4587520 | tf_op jit(solution)/shard_map/all_to_all | solution.py:165
  118.2 5.4 %reshape.917 = f32[128,2,3584]{2,1,0:T(2,128)} reshape(bf16[256,3584]{1,0:T(8,128)(2,1)} %gather_fusion.7) | data formatting | bytes 5505024 | tf_op jit(solution)/shard_map/convert_element_type | solution.py:203
  148.4 5.5 %gather_fusion.1 = bf16[256,3584]{1,0:T(8,128)(2,1)S(1)} fusion(bf16[320,3584]{1,0:T(8,128)(2,1)} %bitcast.11, s32[1024]{0:T(1024)S(1)} %pad_clamp_fusion.8), kind=kCustom, calls=%fused_computation.1 | custom fusion | bytes 3671040 | tf_op jit(solution)/shard_map/gather | solution.py:85
  157.6 8.5 %multiply_reduce_fusion.3 = f32[128,3584]{1,0:T(8,128)} fusion(f32[128,2,3584]{2,1,0:T(2,128)} %reshape.912, f32[128,2]{1,0:T(8,128)S(1)} %copy.87), kind=kLoop, calls=%fused_computation.51 | loop fusion | flops 1376256 | bytes 5506048 | tf_op jit(solution)/shard_map/reduce_sum | solution.py:207
  166.1 6.7 %all-to-all-done.4 = bf16[4,80,3584]{2,1,0:T(8,128)(2,1)} async-done(((bf16[4,80,3584]{2,1,0:T(8,128)(2,1)}), bf16[4,80,3584]{2,1,0:T(8,128)(2,1)}, u32[]{:S(2)}, u32[]{:S(2)}) %all-to-all-start.4) | async-done | bytes 2293792 | tf_op jit(solution)/shard_map/all_to_all | solution.py:179
  172.7 12.3 %fusion.24 = bf16[320,3584]{1,0:T(8,128)(2,1)} fusion(bf16[1,1,3584,1024]{3,2,1,0:T(8,128)(2,1)} %param.20, bf16[320,3584]{1,0:T(8,128)(2,1)} %bitcast.36, bf16[1,1,1024,3584]{3,2,1,0:T(8,128)(2,1)} %param.21, f32[320,1024]{1,0:T(8,128)S(1)} %copy-done.20), kind=kOutput, calls=%fused_computation.36 | convolution fusion | flops 4701716480 | bytes 20578304 | tf_op jit(solution)/shard_map/dot_general | solution.py:56
  197.9 17.2 %all-to-all-done.6 = bf16[4,80,3584]{2,1,0:T(8,128)(2,1)S(1)} async-done(((bf16[4,80,3584]{2,1,0:T(8,128)(2,1)}), bf16[4,80,3584]{2,1,0:T(8,128)(2,1)S(1)}, u32[]{:S(2)}, u32[]{:S(2)}) %all-to-all-start.6) | async-done | bytes 2293792 | tf_op jit(solution)/shard_map/all_to_all | solution.py:194
  218.0 5.2 %reshape.916 = f32[128,2,3584]{2,1,0:T(2,128)} reshape(bf16[256,3584]{1,0:T(8,128)(2,1)} %gather_fusion.6) | data formatting | bytes 5505024 | tf_op jit(solution)/shard_map/convert_element_type | solution.py:110
  223.2 7.7 %reduce_sum.330 = f32[128,3584]{1,0:T(8,128)} reduce(f32[128,2,3584]{2,1,0:T(2,128)} %reshape.916, f32[]{:T(128)} %constant.74.clone.1), dimensions={1}, to_apply=%region_26.27 | reduce | flops 458752 | bytes 5505028 | tf_op jit(solution)/shard_map/reduce_sum | solution.py:110
  243.4 4.9 %all-to-all-start.9 = ((bf16[4,80,3584]{2,1,0:T(8,128)(2,1)}), bf16[4,80,3584]{2,1,0:T(8,128)(2,1)}, u32[]{:S(2)}, u32[]{:S(2)}) async-start(bf16[4,80,3584]{2,1,0:T(8,128)(2,1)} %broadcast_select_fusion), calls=%async_computation.9 | async-start | bytes 4587520 | tf_op jit(solution)/shard_map/all_to_all | solution.py:178
  253.8 21.0 %all-to-all-done.9 = bf16[4,80,3584]{2,1,0:T(8,128)(2,1)} async-done(((bf16[4,80,3584]{2,1,0:T(8,128)(2,1)}), bf16[4,80,3584]{2,1,0:T(8,128)(2,1)}, u32[]{:S(2)}, u32[]{:S(2)}) %all-to-all-start.9) | async-done | bytes 2293792 | tf_op jit(solution)/shard_map/all_to_all | solution.py:178
  281.0 6.3 %fusion.14 = f32[320,1024]{1,0:T(8,128)S(1)} fusion(bf16[320,3584]{1,0:T(8,128)(2,1)} %bitcast.55, bf16[1,1,3584,1024]{3,2,1,0:T(8,128)(2,1)} %param.20), kind=kOutput, calls=%fused_computation.26 | convolution fusion | flops 2348810240 | bytes 10944512 | tf_op jit(solution)/shard_map/dot_general | solution.py:48
  287.4 7.6 %fusion.39 = bf16[320,3584]{1,0:T(8,128)(2,1)} fusion(bf16[1,1,1024,3584]{3,2,1,0:T(8,128)(2,1)} %param.21, f32[320,1024]{1,0:T(8,128)S(1)} %fusion.14), kind=kOutput, calls=%fused_computation.41 | convolution fusion | flops 2351595520 | bytes 10944512 | tf_op jit(solution)/shard_map/dot_general | solution.py:51
  295.0 10.8 %all-to-all-done.2 = bf16[4,80,3584]{2,1,0:T(8,128)(2,1)} async-done(((bf16[4,80,3584]{2,1,0:T(8,128)(2,1)}), bf16[4,80,3584]{2,1,0:T(8,128)(2,1)}, u32[]{:S(2)}, u32[]{:S(2)}) %all-to-all-start.2) | async-done | bytes 2293792 | tf_op jit(solution)/shard_map/all_to_all | solution.py:158
  315.1 5.6 %mul.450 = f32[256,3584]{1,0:T(8,128)} reshape(f32[128,2,3584]{2,1,0:T(2,128)} %mul.449) | data formatting | bytes 7340032 | tf_op jit(solution)/shard_map/mul | solution.py:172
  320.7 12.1 %fusion.33 = bf16[320,3584]{1,0:T(8,128)(2,1)} fusion(bf16[1,1,1024,3584]{3,2,1,0:T(8,128)(2,1)} %param.21, bf16[320,3584]{1,0:T(8,128)(2,1)} %bitcast.20, bf16[1,1,3584,1024]{3,2,1,0:T(8,128)(2,1)} %param.20), kind=kOutput, calls=%fused_computation.39 | convolution fusion | flops 4700405760 | bytes 19267584 | tf_op jit(solution)/shard_map/dot_general | solution.py:44
  343.4 5.4 %reshape.920 = f32[128,2,3584]{2,1,0:T(2,128)} reshape(bf16[256,3584]{1,0:T(8,128)(2,1)} %gather_fusion.11) | data formatting | bytes 5505024 | tf_op jit(solution)/shard_map/convert_element_type | solution.py:203
  372.2 5.5 %gather_fusion.3 = bf16[256,3584]{1,0:T(8,128)(2,1)S(1)} fusion(bf16[320,3584]{1,0:T(8,128)(2,1)} %bitcast.22, s32[1024]{0:T(1024)S(1)} %pad_clamp_fusion.6), kind=kCustom, calls=%fused_computation.3 | custom fusion | bytes 3671040 | tf_op jit(solution)/shard_map/gather | solution.py:85
  381.4 8.5 %multiply_reduce_fusion.2 = f32[128,3584]{1,0:T(8,128)} fusion(f32[128,2,3584]{2,1,0:T(2,128)} %reshape.913, f32[128,2]{1,0:T(8,128)S(1)} %copy.93), kind=kLoop, calls=%fused_computation.50 | loop fusion | flops 1376256 | bytes 5506048 | tf_op jit(solution)/shard_map/reduce_sum | solution.py:207
  390.0 8.0 %all-to-all-done.8 = bf16[4,80,3584]{2,1,0:T(8,128)(2,1)} async-done(((bf16[4,80,3584]{2,1,0:T(8,128)(2,1)}), bf16[4,80,3584]{2,1,0:T(8,128)(2,1)}, u32[]{:S(2)}, u32[]{:S(2)}) %all-to-all-start.8) | async-done | bytes 2293792 | tf_op jit(solution)/shard_map/all_to_all | solution.py:179
  398.0 12.3 %fusion.27 = bf16[320,3584]{1,0:T(8,128)(2,1)} fusion(bf16[1,1,3584,1024]{3,2,1,0:T(8,128)(2,1)} %param.20, bf16[320,3584]{1,0:T(8,128)(2,1)} %bitcast.53, bf16[1,1,1024,3584]{3,2,1,0:T(8,128)(2,1)} %param.21, f32[320,1024]{1,0:T(8,128)S(1)} %copy-done.22), kind=kOutput, calls=%fused_computation.37 | convolution fusion | flops 4701716480 | bytes 20578304 | tf_op jit(solution)/shard_map/dot_general | solution.py:56
  418.6 22.1 %all-to-all-done.10 = bf16[4,80,3584]{2,1,0:T(8,128)(2,1)S(1)} async-done(((bf16[4,80,3584]{2,1,0:T(8,128)(2,1)}), bf16[4,80,3584]{2,1,0:T(8,128)(2,1)S(1)}, u32[]{:S(2)}, u32[]{:S(2)}) %all-to-all-start.10) | async-done | bytes 2293792 | tf_op jit(solution)/shard_map/all_to_all | solution.py:194
  443.6 5.2 %reshape.919 = f32[128,2,3584]{2,1,0:T(2,128)} reshape(bf16[256,3584]{1,0:T(8,128)(2,1)} %gather_fusion.10) | data formatting | bytes 5505024 | tf_op jit(solution)/shard_map/convert_element_type | solution.py:110
  448.8 7.7 %reduce_sum.342 = f32[128,3584]{1,0:T(8,128)} reduce(f32[128,2,3584]{2,1,0:T(2,128)} %reshape.919, f32[]{:T(128)} %constant.74.clone.1), dimensions={1}, to_apply=%region_39.40 | reduce | flops 458752 | bytes 5505028 | tf_op jit(solution)/shard_map/reduce_sum | solution.py:110
  (220 shorter events, 174.5 us)
Async XLA Ops:
  0.6 23.3 %copy-start = (bf16[1,3584,4]{1,2,0:T(4,128)(2,1)S(1)}, bf16[1,3584,4]{1,2,0:T(4,128)(2,1)}, u32[]{:S(2)}) copy-start(bf16[1,3584,4]{1,2,0:T(4,128)(2,1)} %param.19) | copy-start | bytes 86020
  0.6 6.3 %copy-start.13 = (bf16[1,128,3584]{2,1,0:T(8,128)(2,1)S(1)}, bf16[1,128,3584]{2,1,0:T(8,128)(2,1)}, u32[]{:S(2)}) copy-start(bf16[1,128,3584]{2,1,0:T(8,128)(2,1)} %param.11) | copy-start | bytes 2752516
  0.7 6.2 %copy-start.15 = (f32[1,3584]{1,0:T(1,128)S(1)}, f32[1,3584]{1,0:T(1,128)}, u32[]{:S(2)}) copy-start(f32[1,3584]{1,0:T(1,128)} %param.18) | copy-start | bytes 43012
  15.6 5.3 %copy-start.18 = (s32[2,1,128,2]{2,3,1,0:T(2,128)S(1)}, s32[2,1,128,2]{2,3,1,0:T(2,128)}, u32[]{:S(2)}) copy-start(s32[2,1,128,2]{2,3,1,0:T(2,128)} %param.16) | copy-start | bytes 6148
  15.6 33.2 %all-to-all-start.5 = ((bf16[4,80,3584]{2,1,0:T(8,128)(2,1)}), bf16[4,80,3584]{2,1,0:T(8,128)(2,1)}, u32[]{:S(2)}, u32[]{:S(2)}) async-start(bf16[4,80,3584]{2,1,0:T(8,128)(2,1)} %broadcast_select_fusion.2), calls=%async_computation.5 | async-start | bytes 4587520 | tf_op jit(solution)/shard_map/all_to_all | solution.py:178
  30.0 24.1 %copy-start.8 = (f32[128,3584]{1,0:T(8,128)}, f32[128,3584]{1,0:T(8,128)S(1)}, u32[]{:S(2)}) copy-start(f32[128,3584]{1,0:T(8,128)S(1)} %bitcast_convert_fusion) | copy-start | bytes 5505028
  48.8 31.5 %all-to-all-start = ((bf16[4,80,3584]{2,1,0:T(8,128)(2,1)}), bf16[4,80,3584]{2,1,0:T(8,128)(2,1)}, u32[]{:S(2)}, u32[]{:S(2)}) async-start(bf16[4,80,3584]{2,1,0:T(8,128)(2,1)} %broadcast_select_fusion.5), calls=%async_computation | async-start | bytes 4587520 | tf_op jit(solution)/shard_map/all_to_all | solution.py:158
  80.3 30.1 %all-to-all-start.7 = ((bf16[4,80,3584]{2,1,0:T(8,128)(2,1)}), bf16[4,80,3584]{2,1,0:T(8,128)(2,1)S(1)}, u32[]{:S(2)}, u32[]{:S(2)}) async-start(bf16[4,80,3584]{2,1,0:T(8,128)(2,1)} %bitcast.328), calls=%async_computation.7 | async-start | bytes 4587520 | tf_op jit(solution)/shard_map/all_to_all | solution.py:187
  110.4 31.4 %all-to-all-start.1 = ((bf16[4,80,3584]{2,1,0:T(8,128)(2,1)}), bf16[4,80,3584]{2,1,0:T(8,128)(2,1)}, u32[]{:S(2)}, u32[]{:S(2)}) async-start(bf16[4,80,3584]{2,1,0:T(8,128)(2,1)} %bitcast.324), calls=%async_computation.1 | async-start | bytes 4587520 | tf_op jit(solution)/shard_map/all_to_all | solution.py:165
  118.2 5.4 %copy-start.9 = (f32[128,3584]{1,0:T(8,128)S(1)}, f32[128,3584]{1,0:T(8,128)}, u32[]{:S(2)}) copy-start(f32[128,3584]{1,0:T(8,128)} %copy-done.8) | copy-start | bytes 5505028
  141.7 31.0 %all-to-all-start.4 = ((bf16[4,80,3584]{2,1,0:T(8,128)(2,1)}), bf16[4,80,3584]{2,1,0:T(8,128)(2,1)}, u32[]{:S(2)}, u32[]{:S(2)}) async-start(bf16[4,80,3584]{2,1,0:T(8,128)(2,1)} %broadcast_select_fusion.3), calls=%async_computation.4 | async-start | bytes 4587520 | tf_op jit(solution)/shard_map/all_to_all | solution.py:179
  157.6 15.2 %copy-start.20 = (f32[320,1024]{1,0:T(8,128)S(1)}, f32[320,1024]{1,0:T(8,128)}, u32[]{:S(2)}) copy-start(f32[320,1024]{1,0:T(8,128)} %copy-done.19) | copy-start | bytes 3932164
  185.0 30.0 %all-to-all-start.6 = ((bf16[4,80,3584]{2,1,0:T(8,128)(2,1)}), bf16[4,80,3584]{2,1,0:T(8,128)(2,1)S(1)}, u32[]{:S(2)}, u32[]{:S(2)}) async-start(bf16[4,80,3584]{2,1,0:T(8,128)(2,1)} %bitcast.323), calls=%async_computation.6 | async-start | bytes 4587520 | tf_op jit(solution)/shard_map/all_to_all | solution.py:194
  191.3 4.7 %collective-permute-start = (bf16[1,128,3584]{2,1,0:T(8,128)(2,1)}, bf16[1,128,3584]{2,1,0:T(8,128)(2,1)}, u32[]{:S(2)}, u32[]{:S(2)}) collective-permute-start(bf16[1,128,3584]{2,1,0:T(8,128)(2,1)} %fusion.77), channel_id=1, source_target_pairs={{0,4},{4,8},{8,12},{12,16},{16,20},{20,24},{24,28},{1,5},{5,9},{9,... | collective-permute-start | bytes 2752520 | tf_op jit(solution)/shard_map/ppermute | solution.py:17
  197.8 36.2 %copy-start.11 = (bf16[128,3584]{1,0:T(8,128)(2,1)}, bf16[128,3584]{1,0:T(8,128)(2,1)S(1)}, u32[]{:S(2)}) copy-start(bf16[128,3584]{1,0:T(8,128)(2,1)S(1)} %get-tuple-element.29) | copy-start | bytes 2752516
  223.2 7.7 %copy-start.4 = (bf16[2,1,128,3584]{3,2,1,0:T(8,128)(2,1)S(1)}, bf16[2,1,128,3584]{3,2,1,0:T(8,128)(2,1)}, u32[]{:S(2)}) copy-start(bf16[2,1,128,3584]{3,2,1,0:T(8,128)(2,1)} %param.13) | copy-start | bytes 5505028
  230.9 3.1 copy-start.14
  243.4 31.4 %all-to-all-start.9 = ((bf16[4,80,3584]{2,1,0:T(8,128)(2,1)}), bf16[4,80,3584]{2,1,0:T(8,128)(2,1)}, u32[]{:S(2)}, u32[]{:S(2)}) async-start(bf16[4,80,3584]{2,1,0:T(8,128)(2,1)} %broadcast_select_fusion), calls=%async_computation.9 | async-start | bytes 4587520 | tf_op jit(solution)/shard_map/all_to_all | solution.py:178
  253.8 25.5 %copy-start.6 = (bf16[2,1,128,3584]{3,2,1,0:T(8,128)(2,1)S(1)}, bf16[2,1,128,3584]{3,2,1,0:T(8,128)(2,1)}, u32[]{:S(2)}) copy-start(bf16[2,1,128,3584]{3,2,1,0:T(8,128)(2,1)} %param.13) | copy-start | bytes 5505028
  274.8 31.0 %all-to-all-start.2 = ((bf16[4,80,3584]{2,1,0:T(8,128)(2,1)}), bf16[4,80,3584]{2,1,0:T(8,128)(2,1)}, u32[]{:S(2)}, u32[]{:S(2)}) async-start(bf16[4,80,3584]{2,1,0:T(8,128)(2,1)} %broadcast_select_fusion.4), calls=%async_computation.2 | async-start | bytes 4587520 | tf_op jit(solution)/shard_map/all_to_all | solution.py:158
  279.7 29.7 %collective-permute-start.1 = (bf16[1,128,3584]{2,1,0:T(8,128)(2,1)}, bf16[1,128,3584]{2,1,0:T(8,128)(2,1)}, u32[]{:S(2)}, u32[]{:S(2)}) collective-permute-start(bf16[1,128,3584]{2,1,0:T(8,128)(2,1)} %get-tuple-element.31), channel_id=1, source_target_pairs={{4,0},{8,4},{12,8},{16,12},{20,16},{24,20},{28,24},{5,1},{9,5},{13... | collective-permute-start | bytes 2752520 | tf_op jit(solution)/shard_map/ppermute | solution.py:19
  287.3 7.7 %copy-start.21 = (f32[320,1024]{1,0:T(8,128)}, f32[320,1024]{1,0:T(8,128)S(1)}, u32[]{:S(2)}) copy-start(f32[320,1024]{1,0:T(8,128)S(1)} %fusion.14) | copy-start | bytes 3932164
  305.8 30.0 %all-to-all-start.11 = ((bf16[4,80,3584]{2,1,0:T(8,128)(2,1)}), bf16[4,80,3584]{2,1,0:T(8,128)(2,1)S(1)}, u32[]{:S(2)}, u32[]{:S(2)}) async-start(bf16[4,80,3584]{2,1,0:T(8,128)(2,1)} %bitcast.327), calls=%async_computation.11 | async-start | bytes 4587520 | tf_op jit(solution)/shard_map/all_to_all | solution.py:187
  335.8 31.1 %all-to-all-start.3 = ((bf16[4,80,3584]{2,1,0:T(8,128)(2,1)}), bf16[4,80,3584]{2,1,0:T(8,128)(2,1)}, u32[]{:S(2)}, u32[]{:S(2)}) async-start(bf16[4,80,3584]{2,1,0:T(8,128)(2,1)} %bitcast.325), calls=%async_computation.3 | async-start | bytes 4587520 | tf_op jit(solution)/shard_map/all_to_all | solution.py:165
  343.4 5.4 %copy-start.2 = (f32[128,3584]{1,0:T(8,128)S(1)}, f32[128,3584]{1,0:T(8,128)}, u32[]{:S(2)}) copy-start(f32[128,3584]{1,0:T(8,128)} %copy-done.1) | copy-start | bytes 5505028
  362.5 8.9 %copy-start.16 = (s32[1,1,128,2]{2,3,1,0:T(2,128)S(1)}, s32[1,1,128,2]{2,3,1,0:T(2,128)}, u32[]{:S(2)}) copy-start(s32[1,1,128,2]{2,3,1,0:T(2,128)} %get-tuple-element.44) | copy-start | bytes 3076
  362.5 9.5 %copy-start.17 = (s32[128,2]{0,1:T(2,128)S(1)}, s32[128,2]{0,1:T(2,128)}, u32[]{:S(2)}) copy-start(s32[128,2]{0,1:T(2,128)} %get-tuple-element.41) | copy-start | bytes 3076
  366.9 31.0 %all-to-all-start.8 = ((bf16[4,80,3584]{2,1,0:T(8,128)(2,1)}), bf16[4,80,3584]{2,1,0:T(8,128)(2,1)}, u32[]{:S(2)}, u32[]{:S(2)}) async-start(bf16[4,80,3584]{2,1,0:T(8,128)(2,1)} %broadcast_select_fusion.1), calls=%async_computation.8 | async-start | bytes 4587520 | tf_op jit(solution)/shard_map/all_to_all | solution.py:179
  381.4 16.5 %copy-start.22 = (f32[320,1024]{1,0:T(8,128)S(1)}, f32[320,1024]{1,0:T(8,128)}, u32[]{:S(2)}) copy-start(f32[320,1024]{1,0:T(8,128)} %copy-done.21) | copy-start | bytes 3932164
  410.2 4.1 copy-start.12
  410.2 30.4 %all-to-all-start.10 = ((bf16[4,80,3584]{2,1,0:T(8,128)(2,1)}), bf16[4,80,3584]{2,1,0:T(8,128)(2,1)S(1)}, u32[]{:S(2)}, u32[]{:S(2)}) async-start(bf16[4,80,3584]{2,1,0:T(8,128)(2,1)} %bitcast.326), calls=%async_computation.10 | async-start | bytes 4587520 | tf_op jit(solution)/shard_map/all_to_all | solution.py:194
  448.8 7.7 %copy-start.7 = (bf16[2,1,128,3584]{3,2,1,0:T(8,128)(2,1)S(1)}, bf16[2,1,128,3584]{3,2,1,0:T(8,128)(2,1)}, u32[]{:S(2)}) copy-start(bf16[2,1,128,3584]{3,2,1,0:T(8,128)(2,1)} %param.13) | copy-start | bytes 5505028
  (5 other events, 10.2 us)
where the time goes:
time: 470 us; the launch traced here: 463 us
  waiting for transfers between devices  130 us (28%)
  local copies, waits for them, and re-layouts  98.2 us (21%)
  other arithmetic  92.2 us (20%)
  matrix products  84.9 us (18%)
  starting transfers between devices  56.3 us (12%)
    all_to_all x2, waiting for transfers between devices, per_device(): lax.all_to_all(dnormed.reshape(sources, slot_count, model_width), 'expert...  39.2 us
    all_to_all x2, waiting for transfers between devices, per_device(): lax.all_to_all(outgoing_b, 'expert', split_axis=0, concat_axis=0, tiled=T...  37.7 us
    dot_general x2, matrix products, expert_backward(): lax.dot_general(dupward, up_matrix, (((1,), (1,)), ((), ())), preferred_e...  24.6 us
    dot_general x2, matrix products, expert_forward(): jnp.dot(hidden, down_matrix, preferred_element_type=jnp.float32)  24.3 us
    gather x6, local copies, waits for them, and re-layouts, unpack_rows(): return flattened[destination].reshape(token_count, top_count, model_width)  22.8 us
    gather x6, local copies, waits for them, and re-layouts, pack_rows(): taken = jnp.where(filled[:, None], rows[source], jnp.zeros((), rows.dtype))  21.8 us
    mul x4, local copies, waits for them, and re-layouts, per_device(): gate_b[:, :, None] * cotangent.astype(jnp.float32)[:, None, :]  17.5 us
    reduce_sum x2, other arithmetic, per_device(): jnp.sum(gate_f[:, :, None] * expert_f.astype(jnp.float32), axis=1)  17 us
  transfers between devices with their start and end apart: 14, of which 12 were waited for; matrix products, arithmetic and copies ran while one was open for 39% of the time, Pallas kernels for 0%

commit v1 on v0

v1 whole, which is shorter than its diff:
```python
import functools

import jax
import jax.numpy as jnp
from jax import lax
from jax.experimental import pallas as pl
from jax.experimental.pallas import tpu as pltpu
from jax.sharding import PartitionSpec as P

EPSILON = 1e-06
LANES = 128
F32 = jnp.float32
BF16 = jnp.bfloat16
NN = (((1,), (0,)), ((), ()))
NT = (((1,), (1,)), ((), ()))


def mm(a, b, dims=NN, precision=None):
    return lax.dot_general(a, b, dims, preferred_element_type=F32, precision=precision)


def tile_of(extent, most):
    size = most
    while extent % size:
        size -= LANES
    return size


def window_kernel(
    sections,
    experts,
    capacity,
    fwd_state,
    bwd_cot,
    saved,
    fwd_entry,
    bwd_entry,
    fwd_ids,
    fwd_ids_t,
    bwd_ids,
    bwd_ids_t,
    gain,
    router_t,
    up_hbm,
    down_hbm,
    fwd_out,
    bwd_out,
    up_w,
    down_w,
    acts,
    cots,
    stored,
    send_f,
    send_s,
    send_c,
    recv_f,
    recv_s,
    recv_c,
    ret_f,
    ret_g,
    gate_send,
    gate_ret,
    up_buf,
    hid_buf,
    dup_buf,
    scaled_buf,
    load_sems,
    send_sems,
    recv_sems,
    own_sems,
    pipe_send,
    pipe_recv,
    out_sems,
):
    ticks, tokens, width = saved.shape
    top_count = fwd_ids.shape[2]
    hidden_width = up_w.shape[1]
    rows = experts * capacity
    section = lax.axis_index("pipe")
    me = lax.axis_index("expert")
    wide = tile_of(width, 512)
    wide_count = width // wide
    narrow = tile_of(hidden_width, 256)
    narrow_count = hidden_width // narrow

    loads = [
        pltpu.make_async_copy(fwd_state, acts.at[0], load_sems.at[0]),
        pltpu.make_async_copy(bwd_cot, cots.at[0], load_sems.at[1]),
        pltpu.make_async_copy(saved, stored, load_sems.at[2]),
        pltpu.make_async_copy(up_hbm, up_w, load_sems.at[3]),
        pltpu.make_async_copy(down_hbm, down_w, load_sems.at[4]),
    ]
    for load in loads:
        load.start()

    barrier = pltpu.get_barrier_semaphore()
    for offset in range(1, experts):
        pl.semaphore_signal(
            barrier,
            inc=1,
            device_id=(section, lax.rem(me + offset, experts)),
            device_id_type=pl.DeviceIdType.MESH,
        )
    for offset in (1, sections - 1):
        pl.semaphore_signal(
            barrier,
            inc=1,
            device_id=(lax.rem(section + offset, sections), me),
            device_id_type=pl.DeviceIdType.MESH,
        )

    def block_of(index):
        return pl.ds(pl.multiple_of(index * capacity, 16), capacity)

    def exchange(source, target, tick, channel):
        own = pltpu.make_async_copy(
            source.at[block_of(me)], target.at[block_of(me)], own_sems.at[tick, channel]
        )
        copies = []
        for offset in range(1, experts):
            peer = lax.rem(me + offset, experts)
            copies.append(
                pltpu.make_async_remote_copy(
                    src_ref=source.at[block_of(peer)],
                    dst_ref=target.at[block_of(me)],
                    send_sem=send_sems.at[tick, channel, offset - 1],
                    recv_sem=recv_sems.at[tick, channel, offset - 1],
                    device_id=(section, peer),
                    device_id_type=pl.DeviceIdType.MESH,
                )
            )
        for copy in copies:
            copy.start()
        own.start()
        return own, copies

    def arrived(pair):
        pair[0].wait()
        for copy in pair[1]:
            copy.wait_recv()

    def sent(pair):
        for copy in pair[1]:
            copy.wait_send()

    def wide_at(step):
        return pl.ds(pl.multiple_of(step * wide, LANES), wide)

    def narrow_at(step):
        return pl.ds(pl.multiple_of(step * narrow, LANES), narrow)

    def folded(value):
        return sum(value[:, i : i + LANES] for i in range(0, value.shape[1], LANES))

    before = lax.broadcasted_iota(jnp.int32, (tokens, tokens), 0)
    after = lax.broadcasted_iota(jnp.int32, (tokens, tokens), 1)
    lower = jnp.where(after < before, 1.0, 0.0).astype(BF16)
    upper = jnp.where(before < after, 1.0, 0.0).astype(BF16)

    def slots_of(ids_ref, tick):
        ids = ids_ref[tick]
        lane = lax.broadcasted_iota(jnp.int32, (tokens, LANES), 1)
        member = sum(jnp.where(ids[:, k : k + 1] == lane, 1.0, 0.0) for k in range(top_count))
        position = mm(lower, member.astype(BF16))
        base = lane.astype(F32) * float(capacity)
        return member, jnp.where(member > 0.5, position + base, -1.0)

    def packing(ids_t_ref, tick):
        ids = ids_t_ref[tick]
        level = lax.broadcasted_iota(jnp.int32, (16, tokens), 0)
        member = sum(jnp.where(ids[k : k + 1, :] == level, 1.0, 0.0) for k in range(top_count))
        position = mm(member.astype(BF16), upper)
        base = level.astype(F32) * float(capacity)
        slot = jnp.where(member > 0.5, position + base, -1.0)
        row = lax.broadcasted_iota(jnp.int32, (rows, tokens), 0).astype(F32)
        picked = sum(jnp.where(row == slot[e : e + 1, :], 1.0, 0.0) for e in range(experts))
        return picked.astype(BF16)

    def unpacking(slot, weight):
        row = lax.broadcasted_iota(jnp.int32, (tokens, rows), 1).astype(F32)
        return sum(
            jnp.where(row == slot[:, e : e + 1], weight[:, e : e + 1], 0.0)
            for e in range(experts)
        )

    def split_stack(matrix):
        high = matrix.astype(BF16)
        low = (matrix - high.astype(F32)).astype(BF16)
        return jnp.concatenate([high, low], axis=0)

    def inverse_of(act):
        def body(step, total):
            values = act[:, wide_at(step)].astype(F32)
            return total + folded(values * values)

        total = lax.fori_loop(0, wide_count, body, jnp.zeros((tokens, LANES), F32))
        mean = jnp.sum(total, axis=-1, keepdims=True) / float(width)
        return lax.rsqrt(mean + EPSILON)

    def normed_pack(act, inverse, pick, target):
        def body(step, logits):
            at = wide_at(step)
            normed = (act[:, at].astype(F32) * inverse * gain[:, at]).astype(BF16)
            target[:, at] = mm(pick, normed).astype(BF16)
            return logits + mm(normed, router_t[:, at], NT)

        return lax.fori_loop(0, wide_count, body, jnp.zeros((tokens, LANES), F32))

    def plain_pack(act, pick, target):
        def body(step, carry):
            at = wide_at(step)
            target[:, at] = mm(pick, act[:, at]).astype(BF16)
            return carry

        lax.fori_loop(0, wide_count, body, 0)

    def gating(logits, member):
        probability = jax.nn.sigmoid(logits)
        chosen = jnp.where(member > 0.5, probability, 0.0)
        chosen_sum = jnp.sum(chosen, axis=-1, keepdims=True)
        return chosen / chosen_sum, probability, chosen_sum

    def expert_forward(block):
        def up_body(step, carry):
            at = narrow_at(step)
            upward = mm(block[...], up_w[:, at])
            hid_buf[:, at] = (upward * jax.nn.sigmoid(upward)).astype(BF16)
            return carry

        lax.fori_loop(0, narrow_count, up_body, 0)

        def down_body(step, carry):
            at = wide_at(step)
            block[:, at] = mm(hid_buf[...], down_w[:, at]).astype(BF16)
            return carry

        lax.fori_loop(0, wide_count, down_body, 0)

    def expert_up(block):
        def body(step, carry):
            at = narrow_at(step)
            up_buf[:, at] = mm(block[...], up_w[:, at])
            return carry

        lax.fori_loop(0, narrow_count, body, 0)

    def expert_backward(cot_block, target, tick):
        def body(step, total):
            at = narrow_at(step)
            grad = mm(cot_block[...], down_w[at, :], NT)
            upward = up_buf[:, at]
            gate = jax.nn.sigmoid(upward)
            hidden = (upward * gate).astype(BF16).astype(F32)
            dup_buf[:, at] = (grad * gate * (1.0 + upward * (1.0 - gate))).astype(BF16)
            return total + folded(hidden * grad)

        total = lax.fori_loop(0, narrow_count, body, jnp.zeros((rows, LANES), F32))
        gate_grad = jnp.sum(total, axis=-1, keepdims=True)
        lane = lax.broadcasted_iota(jnp.int32, (rows, LANES), 1)
        gate_send[tick] = jnp.where(lane == me, gate_grad, 0.0)

        def back_body(step, carry):
            at = wide_at(step)
            target[:, at] = mm(dup_buf[...], up_w[at, :], NT).astype(BF16)
            return carry

        lax.fori_loop(0, wide_count, back_body, 0)

    def finish_forward(act, back, stack):
        def body(step, carry):
            at = wide_at(step)
            both = mm(stack, back[:, at])
            mixed = act[:, at].astype(F32) + (both[:tokens] + both[tokens:])
            act[:, at] = mixed.astype(BF16)
            return carry

        lax.fori_loop(0, wide_count, body, 0)

    def finish_backward(cot, source, back, gate_back, slot, member, gates, inverse):
        gate, probability, chosen_sum = gates
        stack = split_stack(unpacking(slot, gate))
        plain = unpacking(slot, member)
        gate_grad = mm(plain, gate_back[...], NN, lax.Precision.HIGHEST)
        inner = jnp.sum(gate_grad * gate, axis=-1, keepdims=True)
        chosen_grad = (gate_grad - inner) / chosen_sum
        logit_grad = jnp.where(
            member > 0.5, chosen_grad * probability * (1.0 - probability), 0.0
        )

        def body(step, total):
            at = wide_at(step)
            both = mm(stack, back[:, at])
            grad = both[:tokens] + both[tokens:]
            routing = router_t[0:16, at].astype(F32)
            for e in range(experts):
                grad = grad + logit_grad[:, e : e + 1] * routing[e : e + 1, :]
            scaled = grad * gain[:, at]
            scaled_buf[:, at] = scaled
            return total + folded(scaled * source[:, at].astype(F32))

        total = lax.fori_loop(0, wide_count, body, jnp.zeros((tokens, LANES), F32))
        correction = jnp.sum(total, axis=-1, keepdims=True) / float(width)
        factor = inverse * inverse * inverse * correction

        def last_body(step, carry):
            at = wide_at(step)
            values = source[:, at].astype(F32)
            result = cot[:, at].astype(F32) + inverse * scaled_buf[:, at] - values * factor
            cot[:, at] = result.astype(BF16)
            return carry

        lax.fori_loop(0, wide_count, last_body, 0)

    def start_forward(tick):
        act = acts.at[tick]
        inverse = inverse_of(act)
        logits = normed_pack(act, inverse, packing(fwd_ids_t, tick), send_f)
        return logits

    def forward_stack(tick, logits):
        member, slot = slots_of(fwd_ids, tick)
        gate, _, _ = gating(logits, member)
        return split_stack(unpacking(slot, gate))

    def start_stored(tick):
        act = stored.at[tick]
        inverse = inverse_of(act)
        logits = normed_pack(act, inverse, packing(bwd_ids_t, tick), send_s)
        return inverse, logits

    def end_backward(tick, inverse, logits):
        member, slot = slots_of(bwd_ids, tick)
        gates = gating(logits, member)
        finish_backward(
            cots.at[tick],
            stored.at[tick],
            ret_g,
            gate_ret,
            slot,
            member,
            gates,
            inverse,
        )

    loads[0].wait()
    logits_f = start_forward(0)
    pl.semaphore_wait(barrier, experts + 1)
    trip_f = exchange(send_f, recv_f.at[0], 0, 0)
    loads[2].wait()
    inverse_s, logits_s = start_stored(0)
    trip_s = exchange(send_s, recv_s.at[0], 0, 1)
    loads[1].wait()
    plain_pack(cots.at[0], packing(bwd_ids_t, 0), send_c)
    trip_c = exchange(send_c, recv_c, 0, 2)
    loads[3].wait()
    loads[4].wait()

    outs = []
    for tick in range(ticks):
        more = tick + 1 < ticks
        arrived(trip_f)
        expert_forward(recv_f.at[tick])
        back_f = exchange(recv_f.at[tick], ret_f, tick, 3)
        if tick == 0:
            arrived(trip_s)
            expert_up(recv_s.at[tick])
        arrived(trip_c)
        expert_backward(recv_c, recv_s.at[tick], tick)
        back_g = exchange(recv_s.at[tick], ret_g, tick, 4)
        back_w = exchange(gate_send.at[tick], gate_ret, tick, 5)
        sent(trip_s)
        sent(trip_f)
        sent(trip_c)
        this_inverse, this_logits = inverse_s, logits_s
        if more:
            inverse_s, logits_s = start_stored(tick + 1)
            trip_s = exchange(send_s, recv_s.at[tick + 1], tick + 1, 1)

        arrived(back_f)
        finish_forward(acts.at[tick], ret_f, forward_stack(tick, logits_f))
        outs.append(pltpu.make_async_copy(acts.at[tick], fwd_out.at[tick], out_sems.at[tick, 0]))
        outs[-1].start()
        if more:
            up_hop = pltpu.make_async_remote_copy(
                src_ref=acts.at[tick],
                dst_ref=acts.at[tick + 1],
                send_sem=pipe_send.at[tick, 0],
                recv_sem=pipe_recv.at[tick, 0],
                device_id=(jnp.minimum(section + 1, sections - 1), me),
                device_id_type=pl.DeviceIdType.MESH,
            )
            entry_f = pltpu.make_async_copy(fwd_entry, acts.at[tick + 1], load_sems.at[5])
            pl.when(section < sections - 1)(up_hop.start)
            pl.when(section == 0)(entry_f.start)

        arrived(back_g)
        arrived(back_w)
        end_backward(tick, this_inverse, this_logits)
        outs.append(pltpu.make_async_copy(cots.at[tick], bwd_out.at[tick], out_sems.at[tick, 1]))
        outs[-1].start()
        if more:
            down_hop = pltpu.make_async_remote_copy(
                src_ref=cots.at[tick],
                dst_ref=cots.at[tick + 1],
                send_sem=pipe_send.at[tick, 1],
                recv_sem=pipe_recv.at[tick, 1],
                device_id=(jnp.maximum(section - 1, 0), me),
                device_id_type=pl.DeviceIdType.MESH,
            )
            entry_b = pltpu.make_async_copy(bwd_entry, cots.at[tick + 1], load_sems.at[6])
            pl.when(section > 0)(down_hop.start)
            pl.when(section == sections - 1)(entry_b.start)

            pl.when(section > 0)(up_hop.wait_recv)
            pl.when(section == 0)(entry_f.wait)
            logits_f = start_forward(tick + 1)
            trip_f = exchange(send_f, recv_f.at[tick + 1], tick + 1, 0)
            pl.when(section < sections - 1)(down_hop.wait_recv)
            pl.when(section == sections - 1)(entry_b.wait)
            plain_pack(cots.at[tick + 1], packing(bwd_ids_t, tick + 1), send_c)
            trip_c = exchange(send_c, recv_c, tick + 1, 2)
            arrived(trip_s)
            expert_up(recv_s.at[tick + 1])
            pl.when(section < sections - 1)(up_hop.wait_send)
            pl.when(section > 0)(down_hop.wait_send)
        sent(back_f)
        sent(back_g)
        sent(back_w)
    for out in outs:
        out.wait()


def per_device(
    fwd_state,
    bwd_cot,
    saved_inputs,
    fwd_entry,
    bwd_entry,
    fwd_ids,
    bwd_ids,
    norm_gain,
    router,
    up_weight,
    down_weight,
):
    sections = lax.axis_size("pipe")
    experts = lax.axis_size("expert")
    ticks, _, tokens, width = saved_inputs.shape
    top_count = fwd_ids.shape[3]
    hidden_width = up_weight.shape[3]
    capacity = -(-(5 * tokens * top_count // (4 * experts)) // 16) * 16
    rows = experts * capacity
    router_t = jnp.pad(router[0].T, ((0, LANES - experts), (0, 0)))
    fwd_route, bwd_route = fwd_ids[:, 0], bwd_ids[:, 0]
    anywhere = pl.BlockSpec(memory_space=pl.ANY)
    near = pl.BlockSpec(memory_space=pltpu.VMEM)
    out = jax.ShapeDtypeStruct((ticks, tokens, width), BF16)
    wide_block = pltpu.VMEM((rows, width), BF16)
    tick_block = pltpu.VMEM((ticks, rows, width), BF16)
    token_block = pltpu.VMEM((ticks, tokens, width), BF16)
    small_block = pltpu.VMEM((ticks, rows, LANES), F32)
    forward, backward = pl.pallas_call(
        functools.partial(window_kernel, sections, experts, capacity),
        name="relay_window",
        out_shape=(out, out),
        in_specs=[anywhere] * 5 + [near] * 6 + [anywhere] * 2,
        out_specs=(anywhere, anywhere),
        scratch_shapes=[
            pltpu.VMEM((width, hidden_width), BF16),
            pltpu.VMEM((hidden_width, width), BF16),
            token_block,
            token_block,
            token_block,
            wide_block,
            wide_block,
            wide_block,
            tick_block,
            tick_block,
            wide_block,
            wide_block,
            wide_block,
            small_block,
            pltpu.VMEM((rows, LANES), F32),
            pltpu.VMEM((rows, hidden_width), F32),
            pltpu.VMEM((rows, hidden_width), BF16),
            pltpu.VMEM((rows, hidden_width), BF16),
            pltpu.VMEM((tokens, width), F32),
            pltpu.SemaphoreType.DMA((7,)),
            pltpu.SemaphoreType.DMA((ticks, 6, experts - 1)),
            pltpu.SemaphoreType.DMA((ticks, 6, experts - 1)),
            pltpu.SemaphoreType.DMA((ticks, 6)),
            pltpu.SemaphoreType.DMA((ticks, 2)),
            pltpu.SemaphoreType.DMA((ticks, 2)),
            pltpu.SemaphoreType.DMA((ticks, 2)),
        ],
        compiler_params=pltpu.CompilerParams(
            collective_id=0, has_side_effects=True, vmem_limit_bytes=63 * 1024 * 1024
        ),
    )(
        fwd_state[0],
        bwd_cot[0],
        saved_inputs[:, 0],
        fwd_entry,
        bwd_entry,
        fwd_route,
        jnp.swapaxes(fwd_route, 1, 2),
        bwd_route,
        jnp.swapaxes(bwd_route, 1, 2),
        norm_gain,
        router_t,
        up_weight[0, 0],
        down_weight[0, 0],
    )
    return forward[:, None], backward[:, None]


def solution(mesh):
    placed = (
        P("pipe", "expert", None),
        P("pipe", "expert", None),
        P(None, "pipe", "expert", None),
        P("expert", None),
        P("expert", None),
        P(None, "pipe", "expert", None),
        P(None, "pipe", "expert", None),
        P("pipe", None),
        P("pipe", None, None),
        P("pipe", "expert", None, None),
        P("pipe", "expert", None, None),
    )
    return jax.shard_map(
        per_device,
        mesh=mesh,
        in_specs=placed,
        out_specs=(P(None, "pipe", "expert", None), P(None, "pipe", "expert", None)),
        check_vma=False,
    )
```

time: 470 us -> 274 us (0.58); the launches traced: 463 us -> 274 us
  Pallas kernels: 0 us -> 264 us
  waiting for transfers between devices: 130 us -> 0 us
  other arithmetic: 92.2 us -> 0 us
  local copies, waits for them, and re-layouts: 98.2 us -> 8.88 us
  matrix products: 84.9 us -> 0 us
  starting transfers between devices: 56.3 us -> 0 us
    pallas_call x0 -> x1, Pallas kernels: none -> 264 us  [per_device(): pl.pallas_call(functools.partial(window_kernel, sections, experts, capaci...]
    all_to_all x12 -> x0, waiting for transfers between devices: 130 us -> none  [the longest x2 39.2 us: per_device(): lax.all_to_all(dnormed.reshape(sources, slot_count, model_width), 'expert...]
    dot_general x14 -> x0, matrix products: 84.9 us -> none  [the longest x2 24.6 us: expert_backward(): lax.dot_general(dupward, up_matrix, (((1,), (1,)), ((), ())), preferred_e...]
    all_to_all x12 -> x0, starting transfers between devices: 52.7 us -> none  [the longest x2 10.2 us: per_device(): lax.all_to_all(outgoing_b, 'expert', split_axis=0, concat_axis=0, tiled=T...]
    reduce_sum x25 -> x0, other arithmetic: 46.1 us -> none  [the longest x2 17 us: per_device(): jnp.sum(gate_f[:, :, None] * expert_f.astype(jnp.float32), axis=1)]
    gather x12 -> x0, local copies, waits for them, and re-layouts: 44.5 us -> none  [the longest x6 22.8 us: unpack_rows(): return flattened[destination].reshape(token_count, top_count, model_width)]
    convert_element_type x6 -> x0, local copies, waits for them, and re-layouts: 28.5 us -> none  [the longest x2 10.7 us: per_device(): expert_out.astype(jnp.float32)]
    mul x12 -> x0, local copies, waits for them, and re-layouts: 18.5 us -> none  [the longest x4 17.5 us: per_device(): gate_b[:, :, None] * cotangent.astype(jnp.float32)[:, None, :]]
  transfers between devices with their start and end apart: 14 -> 0, of which waited for: 12 -> 0; matrix products, arithmetic and copies ran while one was open for 39% -> 0% of each run, Pallas kernels for 0% -> 0%
where the time goes in v1:
time: 274 us
  Pallas kernels  264 us (96%)
  local copies, waits for them, and re-layouts  8.88 us (3%)
    pallas_call x1, Pallas kernels, per_device(): pl.pallas_call(functools.partial(window_kernel, sections, experts, capaci...  264 us

profile of v1, /device:TPU:0, one launch (start us, length us, event | category | flops | bytes accessed | tf_op | source)
XLA Modules:
  0.0 274.0 jit_solution(6499661282689379726)
XLA Ops:
  0.6 1.5 copy.14.bwd_ids
  2.1 1.5 copy.13.fwd_ids
  3.6 1.7 pad.4.router_t
  5.3 264.4 %relay_window.1 = (bf16[2,128,3584]{2,1,0:T(8,128)(2,1)}, bf16[2,128,3584]{2,1,0:T(8,128)(2,1)}) custom-call(bf16[128,3584]{1,0:T(8,128)(2,1)} %bitcast.25, bf16[128,3584]{1,0:T(8,128)(2,1)} %bitcast.26, bf16[2,128,3584]{2,1,0:T(8,128)(2,1)} %bitcast.22, bf16[128,3584]{1,0:T(8,128)(2,1)} %fwd_entry.1, bf16[128,3584]{1,0:T(8,128)(2,1)} %bwd_entry.1, ...), custom_call_target="tpu_custom_call" | custom-call | tf_op jit(solution)/shard_map/relay_window/pallas_call | solution.py:462
  269.7 0.0 copy-start
  269.7 3.0 %copy.19 = bf16[2,1,128,3584]{3,2,1,0:T(8,128)(2,1)} copy(bf16[2,1,128,3584]{3,2,1,0:T(8,128)(2,1)} %bitcast.24) | data formatting | bytes 3670016
  272.7 0.0 copy-done
  272.7 1.2 copy.20
Async XLA Ops:
  269.7 3.0 %copy-start = (bf16[2,128,3584]{2,1,0:T(8,128)(2,1)S(1)}, bf16[2,128,3584]{2,1,0:T(8,128)(2,1)}, u32[]{:S(2)}) copy-start(bf16[2,128,3584]{2,1,0:T(8,128)(2,1)} %get-tuple-element.5) | copy-start | bytes 5505028

commit v2 on v1

--- a/solution.py
+++ b/solution.py
@@ -112,17 +112,18 @@
     def block_of(index):
         return pl.ds(pl.multiple_of(index * capacity, 16), capacity)
 
-    def exchange(source, target, tick, channel):
+    def exchange(source, target, tick, channel, at=None, view=None):
+        view = view or (lambda ref, index: ref.at[block_of(index), at or slice(0, width)])
         own = pltpu.make_async_copy(
-            source.at[block_of(me)], target.at[block_of(me)], own_sems.at[tick, channel]
+            view(source, me), view(target, me), own_sems.at[tick, channel]
         )
         copies = []
         for offset in range(1, experts):
             peer = lax.rem(me + offset, experts)
             copies.append(
                 pltpu.make_async_remote_copy(
-                    src_ref=source.at[block_of(peer)],
-                    dst_ref=target.at[block_of(me)],
+                    src_ref=view(source, peer),
+                    dst_ref=view(target, me),
                     send_sem=send_sems.at[tick, channel, offset - 1],
                     recv_sem=recv_sems.at[tick, channel, offset - 1],
                     device_id=(section, peer),
@@ -163,7 +164,11 @@
         member = sum(jnp.where(ids[:, k : k + 1] == lane, 1.0, 0.0) for k in range(top_count))
         position = mm(lower, member.astype(BF16))
         base = lane.astype(F32) * float(capacity)
-        return member, jnp.where(member > 0.5, position + base, -1.0)
+        return (
+            member,
+            jnp.where(member > 0.5, position + base, -1.0),
+            jnp.where(member > 0.5, position, -1.0),
+        )
 
     def packing(ids_t_ref, tick):
         ids = ids_t_ref[tick]
@@ -244,7 +249,7 @@
 
         lax.fori_loop(0, narrow_count, body, 0)
 
-    def expert_backward(cot_block, target, tick):
+    def expert_backward(cot_block, tick):
         def body(step, total):
             at = narrow_at(step)
             grad = mm(cot_block[...], down_w[at, :], NT)
@@ -255,16 +260,28 @@
             return total + folded(hidden * grad)
 
         total = lax.fori_loop(0, narrow_count, body, jnp.zeros((rows, LANES), F32))
-        gate_grad = jnp.sum(total, axis=-1, keepdims=True)
-        lane = lax.broadcasted_iota(jnp.int32, (rows, LANES), 1)
-        gate_send[tick] = jnp.where(lane == me, gate_grad, 0.0)
+        ones = jnp.ones((8, LANES), F32)
+        for source in range(experts):
+            part = total[source * capacity : (source + 1) * capacity]
+            gate_send[tick, source] = jnp.zeros((8, LANES), F32)
+            gate_send[tick, source, :, 0:capacity] = mm(ones, part, NT, lax.Precision.HIGHEST)
 
         def back_body(step, carry):
             at = wide_at(step)
-            target[:, at] = mm(dup_buf[...], up_w[at, :], NT).astype(BF16)
-            return carry
-
-        lax.fori_loop(0, wide_count, back_body, 0)
+            recv_s[tick, :, at] = mm(dup_buf[...], up_w[at, :], NT).astype(BF16)
+            return carry
+
+        return back_body
+
+    def expert_return(body, target, tick):
+        cuts = [0, (wide_count + 1) // 2, wide_count]
+        trips = []
+        for part in range(2):
+            lax.fori_loop(cuts[part], cuts[part + 1], body, 0)
+            at = slice(cuts[part] * wide, cuts[part + 1] * wide)
+            if at.stop > at.start:
+                trips.append(exchange(target, ret_g, tick, 4 + part, at))
+        return trips
 
     def finish_forward(act, back, stack):
         def body(step, carry):
@@ -276,11 +293,15 @@
 
         lax.fori_loop(0, wide_count, body, 0)
 
-    def finish_backward(cot, source, back, gate_back, slot, member, gates, inverse):
+    def finish_backward(cot, source, back, gate_back, ready):
+        stack, member, position, gates, inverse = ready
         gate, probability, chosen_sum = gates
-        stack = split_stack(unpacking(slot, gate))
-        plain = unpacking(slot, member)
-        gate_grad = mm(plain, gate_back[...], NN, lax.Precision.HIGHEST)
+        lane = lax.broadcasted_iota(jnp.int32, (tokens, LANES), 1)
+        gate_grad = jnp.zeros((tokens, LANES), F32)
+        for e in range(experts):
+            named = jnp.where(lane.astype(F32) == position[:, e : e + 1], gate_back[e, 0:1, :], 0.0)
+            value = jnp.sum(named, axis=-1, keepdims=True)
+            gate_grad = jnp.where(lane == e, value, gate_grad)
         inner = jnp.sum(gate_grad * gate, axis=-1, keepdims=True)
         chosen_grad = (gate_grad - inner) / chosen_sum
         logit_grad = jnp.where(
@@ -317,8 +338,8 @@
         logits = normed_pack(act, inverse, packing(fwd_ids_t, tick), send_f)
         return logits
 
-    def forward_stack(tick, logits):
-        member, slot = slots_of(fwd_ids, tick)
+    def forward_ready(tick, logits):
+        member, slot, _ = slots_of(fwd_ids, tick)
         gate, _, _ = gating(logits, member)
         return split_stack(unpacking(slot, gate))
 
@@ -328,19 +349,10 @@
         logits = normed_pack(act, inverse, packing(bwd_ids_t, tick), send_s)
         return inverse, logits
 
-    def end_backward(tick, inverse, logits):
-        member, slot = slots_of(bwd_ids, tick)
+    def backward_ready(tick, inverse, logits):
+        member, slot, position = slots_of(bwd_ids, tick)
         gates = gating(logits, member)
-        finish_backward(
-            cots.at[tick],
-            stored.at[tick],
-            ret_g,
-            gate_ret,
-            slot,
-            member,
-            gates,
-            inverse,
-        )
+        return split_stack(unpacking(slot, gates[0])), member, position, gates, inverse
 
     loads[0].wait()
     logits_f = start_forward(0)
@@ -355,34 +367,38 @@
     loads[3].wait()
     loads[4].wait()
 
+    def own_row(ref, index):
+        return ref.at[index]
+
     outs = []
     for tick in range(ticks):
         more = tick + 1 < ticks
+        act, cot = acts.at[tick], cots.at[tick]
         arrived(trip_f)
         expert_forward(recv_f.at[tick])
-        back_f = exchange(recv_f.at[tick], ret_f, tick, 3)
-        if tick == 0:
-            arrived(trip_s)
-            expert_up(recv_s.at[tick])
+        if more:
+            back_f = exchange(recv_f.at[tick], ret_f, tick, 3)
+        arrived(trip_s)
+        expert_up(recv_s.at[tick])
+        stack_f = forward_ready(tick, logits_f)
+        ready_b = backward_ready(tick, inverse_s, logits_s)
         arrived(trip_c)
-        expert_backward(recv_c, recv_s.at[tick], tick)
-        back_g = exchange(recv_s.at[tick], ret_g, tick, 4)
-        back_w = exchange(gate_send.at[tick], gate_ret, tick, 5)
+        if not more:
+            back_f = exchange(recv_f.at[tick], ret_f, tick, 3)
+        body = expert_backward(recv_c, tick)
+        back_w = exchange(gate_send.at[tick], gate_ret, tick, 6, view=own_row)
+        back_g = expert_return(body, recv_s.at[tick], tick)
         sent(trip_s)
         sent(trip_f)
         sent(trip_c)
-        this_inverse, this_logits = inverse_s, logits_s
         if more:
             inverse_s, logits_s = start_stored(tick + 1)
-            trip_s = exchange(send_s, recv_s.at[tick + 1], tick + 1, 1)
 
         arrived(back_f)
-        finish_forward(acts.at[tick], ret_f, forward_stack(tick, logits_f))
-        outs.append(pltpu.make_async_copy(acts.at[tick], fwd_out.at[tick], out_sems.at[tick, 0]))
-        outs[-1].start()
+        finish_forward(act, ret_f, stack_f)
         if more:
             up_hop = pltpu.make_async_remote_copy(
-                src_ref=acts.at[tick],
+                src_ref=act,
                 dst_ref=acts.at[tick + 1],
                 send_sem=pipe_send.at[tick, 0],
                 recv_sem=pipe_recv.at[tick, 0],
@@ -392,15 +408,23 @@
             entry_f = pltpu.make_async_copy(fwd_entry, acts.at[tick + 1], load_sems.at[5])
             pl.when(section < sections - 1)(up_hop.start)
             pl.when(section == 0)(entry_f.start)
-
-        arrived(back_g)
+        outs.append(pltpu.make_async_copy(act, fwd_out.at[tick], out_sems.at[tick, 0]))
+        outs[-1].start()
+        if more:
+            pl.when(section > 0)(up_hop.wait_recv)
+            pl.when(section == 0)(entry_f.wait)
+            logits_f = start_forward(tick + 1)
+            trip_f = exchange(send_f, recv_f.at[tick + 1], tick + 1, 0)
+
+        for part in back_g:
+            arrived(part)
         arrived(back_w)
-        end_backward(tick, this_inverse, this_logits)
-        outs.append(pltpu.make_async_copy(cots.at[tick], bwd_out.at[tick], out_sems.at[tick, 1]))
-        outs[-1].start()
+        if more:
+            trip_s = exchange(send_s, recv_s.at[tick + 1], tick + 1, 1)
+        finish_backward(cot, stored.at[tick], ret_g, gate_ret, ready_b)
         if more:
             down_hop = pltpu.make_async_remote_copy(
-                src_ref=cots.at[tick],
+                src_ref=cot,
                 dst_ref=cots.at[tick + 1],
                 send_sem=pipe_send.at[tick, 1],
                 recv_sem=pipe_recv.at[tick, 1],
@@ -410,21 +434,18 @@
             entry_b = pltpu.make_async_copy(bwd_entry, cots.at[tick + 1], load_sems.at[6])
             pl.when(section > 0)(down_hop.start)
             pl.when(section == sections - 1)(entry_b.start)
-
-            pl.when(section > 0)(up_hop.wait_recv)
-            pl.when(section == 0)(entry_f.wait)
-            logits_f = start_forward(tick + 1)
-            trip_f = exchange(send_f, recv_f.at[tick + 1], tick + 1, 0)
+        outs.append(pltpu.make_async_copy(cot, bwd_out.at[tick], out_sems.at[tick, 1]))
+        outs[-1].start()
+        if more:
             pl.when(section < sections - 1)(down_hop.wait_recv)
             pl.when(section == sections - 1)(entry_b.wait)
             plain_pack(cots.at[tick + 1], packing(bwd_ids_t, tick + 1), send_c)
             trip_c = exchange(send_c, recv_c, tick + 1, 2)
-            arrived(trip_s)
-            expert_up(recv_s.at[tick + 1])
             pl.when(section < sections - 1)(up_hop.wait_send)
             pl.when(section > 0)(down_hop.wait_send)
         sent(back_f)
-        sent(back_g)
+        for part in back_g:
+            sent(part)
         sent(back_w)
     for out in outs:
         out.wait()
@@ -458,7 +479,7 @@
     wide_block = pltpu.VMEM((rows, width), BF16)
     tick_block = pltpu.VMEM((ticks, rows, width), BF16)
     token_block = pltpu.VMEM((ticks, tokens, width), BF16)
-    small_block = pltpu.VMEM((ticks, rows, LANES), F32)
+    small_block = pltpu.VMEM((ticks, experts, 8, LANES), F32)
     forward, backward = pl.pallas_call(
         functools.partial(window_kernel, sections, experts, capacity),
         name="relay_window",
@@ -480,15 +501,15 @@
             wide_block,
             wide_block,
             small_block,
-            pltpu.VMEM((rows, LANES), F32),
+            pltpu.VMEM((experts, 8, LANES), F32),
             pltpu.VMEM((rows, hidden_width), F32),
             pltpu.VMEM((rows, hidden_width), BF16),
             pltpu.VMEM((rows, hidden_width), BF16),
             pltpu.VMEM((tokens, width), F32),
             pltpu.SemaphoreType.DMA((7,)),
-            pltpu.SemaphoreType.DMA((ticks, 6, experts - 1)),
-            pltpu.SemaphoreType.DMA((ticks, 6, experts - 1)),
-            pltpu.SemaphoreType.DMA((ticks, 6)),
+            pltpu.SemaphoreType.DMA((ticks, 7, experts - 1)),
+            pltpu.SemaphoreType.DMA((ticks, 7, experts - 1)),
+            pltpu.SemaphoreType.DMA((ticks, 7)),
             pltpu.SemaphoreType.DMA((ticks, 2)),
             pltpu.SemaphoreType.DMA((ticks, 2)),
             pltpu.SemaphoreType.DMA((ticks, 2)),

time: 274 us -> 272 us (level)
  no operation moved by 1% of the time
where the time goes in v2:
time: 272 us
  Pallas kernels  262 us (96%)
  local copies, waits for them, and re-layouts  8.88 us (3%)
    pallas_call x1, Pallas kernels, per_device(): pl.pallas_call(functools.partial(window_kernel, sections, experts, capaci...  262 us

profile of v2, /device:TPU:0, one launch (start us, length us, event | category | flops | bytes accessed | tf_op | source)
XLA Modules:
  0.0 271.7 jit_solution(15495270155314955298)
XLA Ops:
  0.6 1.5 copy.14.bwd_ids
  2.1 1.5 copy.13.fwd_ids
  3.6 1.7 pad.4.router_t
  5.3 262.2 %relay_window.1 = (bf16[2,128,3584]{2,1,0:T(8,128)(2,1)}, bf16[2,128,3584]{2,1,0:T(8,128)(2,1)}) custom-call(bf16[128,3584]{1,0:T(8,128)(2,1)} %bitcast.25, bf16[128,3584]{1,0:T(8,128)(2,1)} %bitcast.26, bf16[2,128,3584]{2,1,0:T(8,128)(2,1)} %bitcast.22, bf16[128,3584]{1,0:T(8,128)(2,1)} %fwd_entry.1, bf16[128,3584]{1,0:T(8,128)(2,1)} %bwd_entry.1, ...), custom_call_target="tpu_custom_call" | custom-call | tf_op jit(solution)/shard_map/relay_window/pallas_call | solution.py:483
  267.5 0.0 copy-start
  267.5 3.0 %copy.19 = bf16[2,1,128,3584]{3,2,1,0:T(8,128)(2,1)} copy(bf16[2,1,128,3584]{3,2,1,0:T(8,128)(2,1)} %bitcast.24) | data formatting | bytes 3670016
  270.5 0.0 copy-done
  270.5 1.2 copy.20
Async XLA Ops:
  267.5 3.0 %copy-start = (bf16[2,128,3584]{2,1,0:T(8,128)(2,1)S(1)}, bf16[2,128,3584]{2,1,0:T(8,128)(2,1)}, u32[]{:S(2)}) copy-start(bf16[2,128,3584]{2,1,0:T(8,128)(2,1)} %get-tuple-element.5) | copy-start | bytes 5505028
